TPU v7x, 512 devices: a whole 4x8x8 slice. The times are simulated.
512 devices in a mesh: stn: 16 (over z, core), chan: 32 (over y, x).
Axes of the slice: x: 4, y: 8, z: 8, core: 2. Of those that a mesh axis runs over, the one named last changes fastest.
Arguments:
- voltages: bfloat16 [256, 2048, 512], P('stn', 'chan'), may hold values from -6 to 6
- block_facet: int32 [32, 16, 2048, 1], P('chan', 'stn'), may hold values from 0 to 15; in each aligned block of 2048 rows (0 to 2047, 2048 to 4095, ..., all dimensions but the last counted through in order) at most 192 rows name the same one
- block_tile: int32 [32, 16, 2048], P('chan', 'stn'), may hold values from 0 to 15
- vis_offset: int32 [32, 16, 2048, 128], P('chan', 'stn'), may hold values from 0 to 624
- kernel_taps: bfloat16 [2, 8], replicated, may hold values from 0.19921875 to 1
Outputs:
- image: float32 [2, 2048, 128], P(None, ('stn', 'chan'))
Inputs may be any that keep to these rules, and one draw needn't show every extreme that they name: `block_facet`: among the blocks of one device (one index of the first two dimensions) at most 192 name one facet; in every draw some facet is named by exactly 192 of some device's blocks.
All inputs are finite; a program needn't handle non-finite values.
Results may differ from a plain program's by a relative error of at most 0.0041.
Values may be sent and summed in bfloat16 or wider, within the bound.
A program may use at most 64 MiB of HBM per device.

v0:
```python
import math
import jax
import jax.numpy as jnp
from jax import lax
from jax.sharding import PartitionSpec as P

VB = 128
TILE = 32
KT = 8
TS = 4
TT = 16
OFFS = 25


def kernel_rows(offsets, taps_row):
    cell_ids = jnp.arange(TILE, dtype=jnp.int32)
    distance = cell_ids[None, :, None] - offsets[:, None, :]
    weights_sum = jnp.zeros(distance.shape, jnp.float32)
    for tap_index in range(KT):
        weights_sum = weights_sum + jnp.where(
            distance == tap_index, taps_row[tap_index].astype(jnp.float32), jnp.float32(0.0)
        )
    return weights_sum.astype(jnp.bfloat16)


def block_tiles(values, offsets, kernel_taps):
    along_u = kernel_rows(offsets // OFFS, kernel_taps[0])
    along_v = kernel_rows(offsets % OFFS, kernel_taps[1])
    weighted = (
        values[:, :, None, :].astype(jnp.float32) * along_v[:, None, :, :].astype(jnp.float32)
    ).astype(jnp.bfloat16)
    weighted = weighted.reshape(values.shape[0], 2 * TILE, values.shape[2])
    return jnp.einsum("nux,nwx->nuw", along_u, weighted, preferred_element_type=jnp.float32)


def grid_blocks(values, offsets, target_ids, kernel_taps, segments):
    slot_count = values.shape[0]
    group_size = math.gcd(slot_count, 256)
    tile_width = 2 * TILE * TILE
    segment_ids = jnp.arange(segments, dtype=jnp.int32)

    def accumulate(grids, turn_index):
        first_row = turn_index * group_size
        part_values = lax.dynamic_slice_in_dim(values, first_row, group_size, 0)
        part_offsets = lax.dynamic_slice_in_dim(offsets, first_row, group_size, 0)
        part_targets = lax.dynamic_slice_in_dim(target_ids, first_row, group_size, 0)
        tile_sums = block_tiles(part_values, part_offsets, kernel_taps).reshape(
            group_size, tile_width
        )
        placing = (segment_ids[:, None] == part_targets[None, :]).astype(jnp.float32)
        grids = grids + jnp.dot(
            placing, tile_sums, precision=lax.Precision.HIGHEST, preferred_element_type=jnp.float32
        )
        return (grids, None)

    start_grids = jnp.zeros((segments, tile_width), jnp.float32)
    grids, leftover = lax.scan(accumulate, start_grids, jnp.arange(slot_count // group_size))
    return grids


def facet_grid(tile_grid):
    shaped = tile_grid.reshape(TS, TS, TILE, 2, TILE)
    return jnp.transpose(shaped, (3, 0, 2, 1, 4)).reshape(2, TS * TILE, TS * TILE)


def dft_tables(side):
    index_ids = jnp.arange(side, dtype=jnp.int32)
    phases = index_ids[:, None] * index_ids[None, :] % side
    angles = phases.astype(jnp.float32) * (2.0 * math.pi / side)
    return (jnp.cos(angles), jnp.sin(angles))


def column_pass(grid, cosine, sine):
    high = lax.Precision.HIGHEST
    real_cols = jnp.dot(grid[0], cosine, precision=high) + jnp.dot(grid[1], sine, precision=high)
    imag_cols = jnp.dot(grid[1], cosine, precision=high) - jnp.dot(grid[0], sine, precision=high)
    return (real_cols, imag_cols)


def row_pass(real_cols, imag_cols, cosine_rows, sine_rows):
    high = lax.Precision.HIGHEST
    real_rows = jnp.dot(cosine_rows, real_cols, precision=high) + jnp.dot(
        sine_rows, imag_cols, precision=high
    )
    imag_rows = jnp.dot(cosine_rows, imag_cols, precision=high) - jnp.dot(
        sine_rows, real_cols, precision=high
    )
    return (real_rows, imag_rows)


def body(voltages, block_facet, block_tile, vis_offset, kernel_taps):
    facets = lax.axis_size("stn")
    chan_count = lax.axis_size("chan")
    panels = lax.all_to_all(voltages, "stn", split_axis=1, concat_axis=0, tiled=True)
    stations = panels.shape[0]
    local_channels = panels.shape[1]
    samples = panels.shape[2] // 2
    swapped = jnp.concatenate([panels[:, :, samples:], -panels[:, :, :samples]], axis=2)
    stacked = jnp.concatenate([panels, swapped], axis=0)
    products = jnp.einsum("aks,jks->kaj", stacked, panels, preferred_element_type=jnp.float32)
    station_ids = jnp.arange(stations, dtype=jnp.int32)
    off_diagonal = (station_ids[:, None] != station_ids[None, :]).astype(jnp.float32)
    scale = 1.0 / math.sqrt(samples)
    real_vis = (products[:, :stations, :] * scale * off_diagonal).astype(jnp.bfloat16)
    imag_vis = (products[:, stations:, :] * scale * off_diagonal).astype(jnp.bfloat16)
    block_values = jnp.stack([real_vis.reshape(-1, VB), imag_vis.reshape(-1, VB)], axis=1)
    block_count = block_values.shape[0]
    offsets = vis_offset.reshape(block_count, VB)
    tile_ids = block_tile.reshape(block_count)
    facet_ids = block_facet.reshape(block_count)
    capacity = 3 * block_count // (2 * facets)
    facet_range = jnp.arange(facets, dtype=jnp.int32)
    member = (facet_ids[:, None] == facet_range[None, :]).astype(jnp.int32)
    earlier = jnp.cumsum(member, axis=0) - member
    position = jnp.sum(earlier * member, axis=1)
    slot_ids = facet_ids * capacity + position
    send_values = jnp.zeros((facets * capacity, 2, VB), jnp.bfloat16).at[slot_ids].set(block_values)
    send_offsets = jnp.zeros((facets * capacity, VB), jnp.int32).at[slot_ids].set(offsets)
    send_tiles = jnp.zeros((facets * capacity,), jnp.int32).at[slot_ids].set(tile_ids)
    got_values, got_offsets, got_tiles = (
        lax.all_to_all(send_values, "stn", split_axis=0, concat_axis=0, tiled=True),
        lax.all_to_all(send_offsets, "stn", split_axis=0, concat_axis=0, tiled=True),
        lax.all_to_all(send_tiles, "stn", split_axis=0, concat_axis=0, tiled=True),
    )
    tile_grid = grid_blocks(got_values, got_offsets, got_tiles, kernel_taps, TT)
    grid = facet_grid(tile_grid)
    side = grid.shape[1]
    row_count = side // chan_count
    channels_all = local_channels * facets * chan_count
    norm_factor = 1.0 / math.sqrt(channels_all * stations * stations * KT * KT / facets)
    cosine, sine = dft_tables(side)
    summed = lax.psum(grid, "chan")
    real_cols, imag_cols = column_pass(summed, cosine, sine)
    first_row = lax.axis_index("chan") * row_count
    cosine_rows = lax.dynamic_slice_in_dim(cosine, first_row, row_count, 0)
    sine_rows = lax.dynamic_slice_in_dim(sine, first_row, row_count, 0)
    real_rows, imag_rows = row_pass(real_cols, imag_cols, cosine_rows, sine_rows)
    image = jnp.stack([real_rows, imag_rows], axis=0) * norm_factor
    return image


def solution(mesh):
    placed = (
        P("stn", "chan", None),
        P("chan", "stn", None, None),
        P("chan", "stn", None),
        P("chan", "stn", None, None),
        P(),
    )
    return jax.shard_map(
        body, mesh=mesh, in_specs=placed, out_specs=P(None, ("stn", "chan"), None), check_vma=False
    )
```

profile of v0, /device:TPU:2, one launch (start us, length us, event | category | flops | bytes accessed | tf_op | source)
XLA Modules:
  0.0 876.2 jit_solution(455187938880387183)
XLA Ops:
  7.3 4.5 reduce-window.6
  14.1 8.2 scatter_custom_fusion
  23.0 10.4 %all-to-all-start = ((s32[16,192,1]{1,2,0:T(1,128)}), s32[16,192,1]{1,2,0:T(1,128)S(1)}, u32[]{:S(2)}, u32[]{:S(2)}) async-start(s32[16,192,1]{1,2,0:T(1,128)} %all_to_all.43), calls=%async_computation | async-start | bytes 32768 | tf_op jit(solution)/shard_map/all_to_all | solution.py:123
  36.2 4.9 all-to-all-done
  44.7 6.8 scatter_custom_fusion.1
  51.6 19.8 %all-to-all-done.2 = bf16[16,64,512]{2,0,1:T(8,128)(2,1)S(1)} async-done(((bf16[16,64,512]{2,0,1:T(8,128)(2,1)}), bf16[16,64,512]{2,0,1:T(8,128)(2,1)S(1)}, u32[]{:S(2)}, u32[]{:S(2)}) %all-to-all-start.2) | async-done | bytes 1048608 | tf_op jit(solution)/shard_map/all_to_all | solution.py:94
  71.3 4.8 all-to-all-start.1
  84.7 185.7 %scatter_fusion = bf16[3072,2,128]{2,1,0:T(2,128)(2,1)} fusion(bf16[3072,2,128]{2,1,0:T(2,128)(2,1)} %broadcast_in_dim.128, s32[2048]{0:T(1024)S(1)} %bitcast.146, bf16[2048,2,128]{2,1,0:T(2,128)(2,1)S(1)} %pad_maximum_fusion), kind=kCustom, calls=%fused_computation.2 | custom fusion | bytes 3153920 | tf_op jit(solution)/shard_map/scatter | solution.py:117
  270.4 7.3 all-to-all-start.3
  278.0 37.6 %all-to-all-done.3 = bf16[3072,2,128]{2,1,0:T(2,128)(2,1)} async-done(((bf16[3072,2,128]{2,1,0:T(2,128)(2,1)}), bf16[3072,2,128]{2,1,0:T(2,128)(2,1)}, u32[]{:S(2)}, u32[]{:S(2)}) %all-to-all-start.3) | async-done | bytes 1572896 | tf_op jit(solution)/shard_map/all_to_all | solution.py:121
  315.6 394.3 %while.13 = (s32[]{:T(128)}, f32[16,2048]{1,0:T(8,128)S(1)}, s32[12]{0:T(128)S(1)}, s32[3072]{0:T(1024)S(1)}, s32[3072,128]{1,0:T(8,128)}, /*index=5*/bf16[2,8]{...) while((s32[]{:T(128)}, f32[16,2048]{1,0:T(8,128)S(1)}, ...), condition=%wide.region_7.8_spmd.clone, body=%wide.region_6.7_spmd.clone.sunk | while | flops 293081088 | bytes 26742172 | solution.py:57
  336.1 7.6 fusion.128
  368.9 7.6 fusion.128
  401.8 7.6 fusion.128
  434.6 7.6 fusion.128
  467.5 7.6 fusion.128
  500.3 7.6 fusion.128
  533.2 7.6 fusion.128
  566.0 7.6 fusion.128
  598.9 7.6 fusion.128
  631.7 7.6 fusion.128
  664.5 7.6 fusion.128
  697.4 7.6 fusion.128
  712.2 150.7 %all-reduce.2.cloned.1.call-done = f32[2,128,128]{2,1,0:T(8,128)} async-done(((f32[2,128,128]{2,1,0:T(8,128)}), f32[2,128,128]{2,1,0:T(8,128)}) %all-reduce.2.cloned.1.call-update) | async-done | bytes 131088 | tf_op jit(solution)/shard_map/psum | solution.py:132
  (151 shorter events, 202.3 us)
Async XLA Ops:
  6.5 38.2 %copy-start = (s32[1,1,2048,128]{3,2,1,0:T(8,128)S(1)}, s32[1,1,2048,128]{3,2,1,0:T(8,128)}, u32[]{:S(2)}) copy-start(s32[1,1,2048,128]{3,2,1,0:T(8,128)} %param.10) | copy-start | bytes 3145732
  23.0 18.1 %all-to-all-start = ((s32[16,192,1]{1,2,0:T(1,128)}), s32[16,192,1]{1,2,0:T(1,128)S(1)}, u32[]{:S(2)}, u32[]{:S(2)}) async-start(s32[16,192,1]{1,2,0:T(1,128)} %all_to_all.43), calls=%async_computation | async-start | bytes 32768 | tf_op jit(solution)/shard_map/all_to_all | solution.py:123
  41.1 30.3 %all-to-all-start.2 = ((bf16[16,64,512]{2,0,1:T(8,128)(2,1)}), bf16[16,64,512]{2,0,1:T(8,128)(2,1)S(1)}, u32[]{:S(2)}, u32[]{:S(2)}) async-start(bf16[16,64,512]{2,0,1:T(8,128)(2,1)} %copy.16), calls=%async_computation.2 | async-start | bytes 2097152 | tf_op jit(solution)/shard_map/all_to_all | solution.py:94
  71.3 199.0 %all-to-all-start.1 = ((s32[16,192,128]{2,1,0:T(8,128)}), s32[16,192,128]{2,1,0:T(8,128)}, u32[]{:S(2)}, u32[]{:S(2)}) async-start(s32[16,192,128]{2,1,0:T(8,128)} %bitcast.8), calls=%async_computation.1 | async-start | bytes 3145728 | tf_op jit(solution)/shard_map/all_to_all | solution.py:122
  82.5 233.0 %copy-start.1 = (bf16[2,8]{1,0:T(2,128)(2,1)S(1)}, bf16[2,8]{1,0:T(2,128)(2,1)}, u32[]{:S(2)}) copy-start(bf16[2,8]{1,0:T(2,128)(2,1)} %param.11) | copy-start | bytes 100
  270.4 45.2 %all-to-all-start.3 = ((bf16[3072,2,128]{2,1,0:T(2,128)(2,1)}), bf16[3072,2,128]{2,1,0:T(2,128)(2,1)}, u32[]{:S(2)}, u32[]{:S(2)}) async-start(bf16[3072,2,128]{2,1,0:T(2,128)(2,1)} %scatter_fusion), calls=%async_computation.3 | async-start | bytes 3145728 | tf_op jit(solution)/shard_map/all_to_all | solution.py:121
  277.6 585.3 %all-reduce.2.cloned.1.call-start = ((), (), s32[]{:S(2)}) async-start(), calls=%async_computation.4 | async-start | bytes 262144 | tf_op jit(solution)/shard_map/psum | solution.py:132
Sparse Core Ops, SparseCore 0:
  711.7 151.1 all-reduce.1
where the time goes:
time: 881 us; the launch traced here: 876 us
  local copies, waits for them, and re-layouts  271 us (31%)
  waiting for transfers between devices  213 us (24%)
  loops' own time  128 us (15%)
  other arithmetic  114 us (13%)
  matrix products  111 us (13%)
  starting transfers between devices  26.4 us (3%)
  between operations  13.6 us (2%)
    scatter x1, local copies, waits for them, and re-layouts, body(): jnp.zeros((facets * capacity, 2, VB), jnp.bfloat16).at[slot_ids]  186 us
    psum x1, waiting for transfers between devices, body(): summed = lax.psum(grid, 'chan')  151 us
    another operation x1, loops' own time, grid_blocks(): lax.scan(accumulate, start_grids, jnp.arange(slot_count // group_size))  128 us
    dot_general x12, matrix products, block_tiles(): jnp.einsum('nux,nwx->nuw', along_u, weighted, preferred_element_type=jnp....  91.5 us
    dot_general x12, local copies, waits for them, and re-layouts, block_tiles(): jnp.einsum('nux,nwx->nuw', along_u, weighted, preferred_element_type=jnp....  42.5 us
    convert_element_type x12, other arithmetic, block_tiles(): along_v[:, None, :, :].astype(jnp.float32)  38.9 us
    convert_element_type x12, other arithmetic, block_tiles(): weighted = (values[:, :, None, :].astype(jnp.float32) * along_v[:, None,...  38.3 us
    all_to_all x1, waiting for transfers between devices, body(): lax.all_to_all(send_values, 'stn', split_axis=0, concat_axis=0, tiled=True)  37.6 us
  transfers between devices with their start and end apart: 5, of which 4 were waited for; matrix products, arithmetic and copies ran while one was open for 23% of the time, Pallas kernels for 0%

commit v1 on v0

--- a/solution.py
+++ b/solution.py
@@ -10,6 +10,22 @@
 TS = 4
 TT = 16
 OFFS = 25
+
+
+def pairwise_exchange(value, axis, split, join):
+    ways, here = (lax.axis_size(axis), lax.axis_index(axis))
+    width = value.shape[split] // ways
+    lengths = list(value.shape)
+    lengths[split] = width
+    height = lengths[join]
+    lengths[join] = height * ways
+    full = jnp.zeros(lengths, value.dtype)
+    for mask in range(ways):
+        part = lax.dynamic_slice_in_dim(value, (here ^ mask) * width, width, axis=split)
+        if mask:
+            part = lax.ppermute(part, axis, [(d, d ^ mask) for d in range(ways)])
+        full = lax.dynamic_update_slice_in_dim(full, part, (here ^ mask) * height, axis=join)
+    return full
 
 
 def kernel_rows(offsets, taps_row):
@@ -118,7 +134,7 @@
     send_offsets = jnp.zeros((facets * capacity, VB), jnp.int32).at[slot_ids].set(offsets)
     send_tiles = jnp.zeros((facets * capacity,), jnp.int32).at[slot_ids].set(tile_ids)
     got_values, got_offsets, got_tiles = (
-        lax.all_to_all(send_values, "stn", split_axis=0, concat_axis=0, tiled=True),
+        pairwise_exchange(send_values, "stn", 0, 0),
         lax.all_to_all(send_offsets, "stn", split_axis=0, concat_axis=0, tiled=True),
         lax.all_to_all(send_tiles, "stn", split_axis=0, concat_axis=0, tiled=True),
     )

time: 881 us -> 839 us (0.952)
  local copies, waits for them, and re-layouts: 271 us -> 217 us
  starting transfers between devices: 26.4 us -> 76.1 us
  waiting for transfers between devices: 213 us -> 168 us
    scatter x1, local copies, waits for them, and re-layouts: 186 us -> 118 us  [body(): jnp.zeros((facets * capacity, 2, VB), jnp.bfloat16).at[slot_ids]]
    ppermute x0 -> x15, starting transfers between devices: none -> 54.2 us  [pairwise_exchange(): part = lax.ppermute(part, axis, [(d, d ^ mask) for d in range(ways)])]
    all_to_all x1 -> x0, waiting for transfers between devices: 37.6 us -> none  [body(): lax.all_to_all(send_values, 'stn', split_axis=0, concat_axis=0, tiled=True)]
    dynamic_update_slice x0 -> x15, local copies, waits for them, and re-layouts: none -> 10.7 us  [pairwise_exchange(): lax.dynamic_update_slice_in_dim(full, part, (here ^ mask) * height, axis=...]
  transfers between devices with their start and end apart: 5 -> 19, of which waited for: 4 -> 5; matrix products, arithmetic and copies ran while one was open for 23% -> 20% of each run, Pallas kernels for 0% -> 0%
where the time goes in v1:
time: 839 us; the launch traced here: 829 us
  local copies, waits for them, and re-layouts  217 us (26%)
  waiting for transfers between devices  168 us (20%)
  loops' own time  131 us (16%)
  other arithmetic  112 us (13%)
  matrix products  111 us (13%)
  starting transfers between devices  76.1 us (9%)
  between operations  13.9 us (2%)
    psum x1, waiting for transfers between devices, body(): summed = lax.psum(grid, 'chan')  151 us
    another operation x1, loops' own time, grid_blocks(): lax.scan(accumulate, start_grids, jnp.arange(slot_count // group_size))  131 us
    scatter x1, local copies, waits for them, and re-layouts, body(): jnp.zeros((facets * capacity, 2, VB), jnp.bfloat16).at[slot_ids]  118 us
    dot_general x12, matrix products, block_tiles(): jnp.einsum('nux,nwx->nuw', along_u, weighted, preferred_element_type=jnp....  91.6 us
    ppermute x15, starting transfers between devices, pairwise_exchange(): part = lax.ppermute(part, axis, [(d, d ^ mask) for d in range(ways)])  54.2 us
    dot_general x12, local copies, waits for them, and re-layouts, block_tiles(): jnp.einsum('nux,nwx->nuw', along_u, weighted, preferred_element_type=jnp....  42.5 us
    convert_element_type x12, other arithmetic, block_tiles(): along_v[:, None, :, :].astype(jnp.float32)  38.9 us
    convert_element_type x12, other arithmetic, block_tiles(): weighted = (values[:, :, None, :].astype(jnp.float32) * along_v[:, None,...  38.6 us
  transfers between devices with their start and end apart: 19, of which 5 were waited for; matrix products, arithmetic and copies ran while one was open for 20% of the time, Pallas kernels for 0%

profile of v1, /device:TPU:2, one launch (start us, length us, event | category | flops | bytes accessed | tf_op | source)
XLA Modules:
  0.0 829.3 jit_solution(5838611937350696184)
XLA Ops:
  9.4 10.4 %all-to-all-start.2 = ((bf16[16,64,512]{2,0,1:T(8,128)(2,1)}), bf16[16,64,512]{2,0,1:T(8,128)(2,1)S(1)}, u32[]{:S(2)}, u32[]{:S(2)}) async-start(bf16[16,64,512]{2,0,1:T(8,128)(2,1)} %copy.16), calls=%async_computation.2 | async-start | bytes 2097152 | tf_op jit(solution)/shard_map/all_to_all | solution.py:110
  25.2 8.2 scatter_custom_fusion
  34.2 12.4 %all-to-all-done.2 = bf16[16,64,512]{2,0,1:T(8,128)(2,1)S(1)} async-done(((bf16[16,64,512]{2,0,1:T(8,128)(2,1)}), bf16[16,64,512]{2,0,1:T(8,128)(2,1)S(1)}, u32[]{:S(2)}, u32[]{:S(2)}) %all-to-all-start.2) | async-done | bytes 1048608 | tf_op jit(solution)/shard_map/all_to_all | solution.py:110
  46.5 4.8 all-to-all-start
  51.4 6.8 scatter_custom_fusion.1
  58.9 6.7 all-to-all-start.1
  75.2 117.7 %scatter_fusion = bf16[3072,2,128]{2,1,0:T(2,128)(2,1)S(1)} fusion(bf16[3072,2,128]{2,1,0:T(2,128)(2,1)S(1)} %broadcast.315.clone, s32[2048]{0:T(1024)S(1)} %bitcast.146, bf16[2048,2,128]{2,1,0:T(2,128)(2,1)} %pad_maximum_fusion), kind=kCustom, calls=%fused_computation.2 | custom fusion | bytes 3153920 | tf_op jit(solution)/shard_map/scatter | solution.py:133
  211.4 5.4 collective-permute-start.5
  220.2 7.5 collective-permute-start.7
  250.2 4.8 collective-permute-start.13
  266.5 396.7 %while.13 = (s32[]{:T(128)}, f32[16,2048]{1,0:T(8,128)S(1)}, s32[12]{0:T(128)S(1)}, s32[3072]{0:T(1024)S(1)}, s32[3072,128]{1,0:T(8,128)}, /*index=5*/bf16[2,8]{...) while((s32[]{:T(128)}, f32[16,2048]{1,0:T(8,128)S(1)}, ...), condition=%wide.region_7.8_spmd.clone, body=%wide.region_6.7_spmd.clone.sunk | while | flops 293081088 | bytes 26742172 | solution.py:73
  287.2 7.6 fusion.120
  320.3 7.6 fusion.120
  353.3 7.6 fusion.120
  386.4 7.6 fusion.120
  419.4 7.6 fusion.120
  452.4 7.6 fusion.120
  485.5 7.6 fusion.120
  518.5 7.6 fusion.120
  551.6 7.6 fusion.120
  584.6 7.6 fusion.120
  617.7 7.6 fusion.120
  650.7 7.6 fusion.120
  665.5 150.5 %all-reduce.2.cloned.1.call-done = f32[2,128,128]{2,1,0:T(8,128)} async-done(((f32[2,128,128]{2,1,0:T(8,128)}), f32[2,128,128]{2,1,0:T(8,128)}) %all-reduce.2.cloned.1.call-update) | async-done | bytes 131088 | tf_op jit(solution)/shard_map/psum | solution.py:148
  (200 shorter events, 257.8 us)
Async XLA Ops:
  6.5 44.9 %copy-start = (s32[1,1,2048,128]{3,2,1,0:T(8,128)S(1)}, s32[1,1,2048,128]{3,2,1,0:T(8,128)}, u32[]{:S(2)}) copy-start(s32[1,1,2048,128]{3,2,1,0:T(8,128)} %param.10) | copy-start | bytes 3145732
  6.5 13.3 %copy-start.3 = (s32[1,1,2048,1]{2,3,1,0:T(1,128)S(1)}, s32[1,1,2048,1]{2,3,1,0:T(1,128)}, u32[]{:S(2)}) copy-start(s32[1,1,2048,1]{2,3,1,0:T(1,128)} %param.8) | copy-start | bytes 24580
  9.4 37.1 %all-to-all-start.2 = ((bf16[16,64,512]{2,0,1:T(8,128)(2,1)}), bf16[16,64,512]{2,0,1:T(8,128)(2,1)S(1)}, u32[]{:S(2)}, u32[]{:S(2)}) async-start(bf16[16,64,512]{2,0,1:T(8,128)(2,1)} %copy.16), calls=%async_computation.2 | async-start | bytes 2097152 | tf_op jit(solution)/shard_map/all_to_all | solution.py:110
  46.5 12.4 %all-to-all-start = ((s32[16,192,1]{1,2,0:T(1,128)}), s32[16,192,1]{1,2,0:T(1,128)S(1)}, u32[]{:S(2)}, u32[]{:S(2)}) async-start(s32[16,192,1]{1,2,0:T(1,128)} %all_to_all.39), calls=%async_computation | async-start | bytes 32768 | tf_op jit(solution)/shard_map/all_to_all | solution.py:139
  58.9 207.6 %all-to-all-start.1 = ((s32[16,192,128]{2,1,0:T(8,128)}), s32[16,192,128]{2,1,0:T(8,128)}, u32[]{:S(2)}, u32[]{:S(2)}) async-start(s32[16,192,128]{2,1,0:T(8,128)} %bitcast.8), calls=%async_computation.1 | async-start | bytes 3145728 | tf_op jit(solution)/shard_map/all_to_all | solution.py:138
  65.7 750.4 %all-reduce.2.cloned.1.call-start = ((), (), s32[]{:S(2)}) async-start(), calls=%async_computation.3 | async-start | bytes 262144 | tf_op jit(solution)/shard_map/psum | solution.py:148
  192.9 73.6 %copy-start.1 = (bf16[2,8]{1,0:T(2,128)(2,1)S(1)}, bf16[2,8]{1,0:T(2,128)(2,1)}, u32[]{:S(2)}) copy-start(bf16[2,8]{1,0:T(2,128)(2,1)} %param.11) | copy-start | bytes 100
  195.8 1.1 copy-start.2
  197.0 14.4 %collective-permute-start = (bf16[192,2,128]{2,1,0:T(2,128)(2,1)}, bf16[192,2,128]{2,1,0:T(2,128)(2,1)S(1)}, u32[]{:S(2)}, u32[]{:S(2)}) collective-permute-start(bf16[192,2,128]{2,1,0:T(2,128)(2,1)} %get-tuple-element.184), channel_id=1, source_target_pairs={{0,32},{32,0},{64,96},{96,64},{128,160},{160,128},{192,224},{224,1... | collective-permute-start | bytes 294920 | tf_op jit(solution)/shard_map/ppermute | solution.py:26
  199.4 18.2 %collective-permute-start.1 = (bf16[192,2,128]{2,1,0:T(2,128)(2,1)}, bf16[192,2,128]{2,1,0:T(2,128)(2,1)S(1)}, u32[]{:S(2)}, u32[]{:S(2)}) collective-permute-start(bf16[192,2,128]{2,1,0:T(2,128)(2,1)} %get-tuple-element.183), channel_id=1, source_target_pairs={{0,64},{32,96},{64,0},{96,32},{128,192},{160,224},{192,128},{224,1... | collective-permute-start | bytes 294920 | tf_op jit(solution)/shard_map/ppermute | solution.py:26
  202.9 17.2 %collective-permute-start.2 = (bf16[192,2,128]{2,1,0:T(2,128)(2,1)}, bf16[192,2,128]{2,1,0:T(2,128)(2,1)S(1)}, u32[]{:S(2)}, u32[]{:S(2)}) collective-permute-start(bf16[192,2,128]{2,1,0:T(2,128)(2,1)} %get-tuple-element.182), channel_id=1, source_target_pairs={{0,96},{32,64},{64,32},{96,0},{128,224},{160,192},{192,160},{224,1... | collective-permute-start | bytes 294920 | tf_op jit(solution)/shard_map/ppermute | solution.py:26
  204.9 23.5 %collective-permute-start.3 = (bf16[192,2,128]{2,1,0:T(2,128)(2,1)}, bf16[192,2,128]{2,1,0:T(2,128)(2,1)S(1)}, u32[]{:S(2)}, u32[]{:S(2)}) collective-permute-start(bf16[192,2,128]{2,1,0:T(2,128)(2,1)} %get-tuple-element.181), channel_id=1, source_target_pairs={{0,128},{32,160},{64,192},{96,224},{128,0},{160,32},{192,64},{224,... | collective-permute-start | bytes 294920 | tf_op jit(solution)/shard_map/ppermute | solution.py:26
  209.4 21.7 %collective-permute-start.4 = (bf16[192,2,128]{2,1,0:T(2,128)(2,1)}, bf16[192,2,128]{2,1,0:T(2,128)(2,1)S(1)}, u32[]{:S(2)}, u32[]{:S(2)}) collective-permute-start(bf16[192,2,128]{2,1,0:T(2,128)(2,1)} %get-tuple-element.180), channel_id=1, source_target_pairs={{0,160},{32,128},{64,224},{96,192},{128,32},{160,0},{192,96},{224,... | collective-permute-start | bytes 294920 | tf_op jit(solution)/shard_map/ppermute | solution.py:26
  211.4 25.2 %collective-permute-start.5 = (bf16[192,2,128]{2,1,0:T(2,128)(2,1)}, bf16[192,2,128]{2,1,0:T(2,128)(2,1)S(1)}, u32[]{:S(2)}, u32[]{:S(2)}) collective-permute-start(bf16[192,2,128]{2,1,0:T(2,128)(2,1)} %get-tuple-element.179), channel_id=1, source_target_pairs={{0,192},{32,224},{64,128},{96,160},{128,64},{160,96},{192,0},{224,... | collective-permute-start | bytes 294920 | tf_op jit(solution)/shard_map/ppermute | solution.py:26
  217.5 23.5 %collective-permute-start.6 = (bf16[192,2,128]{2,1,0:T(2,128)(2,1)S(1)}, bf16[192,2,128]{2,1,0:T(2,128)(2,1)S(1)}, u32[]{:S(2)}, u32[]{:S(2)}) collective-permute-start(bf16[192,2,128]{2,1,0:T(2,128)(2,1)S(1)} %get-tuple-element.178), channel_id=1, source_target_pairs={{0,224},{32,192},{64,160},{96,128},{128,96},{160,64},{192,32},{224... | collective-permute-start | bytes 294920 | tf_op jit(solution)/shard_map/ppermute | solution.py:26
  220.2 25.5 %collective-permute-start.7 = (bf16[192,2,128]{2,1,0:T(2,128)(2,1)S(1)}, bf16[192,2,128]{2,1,0:T(2,128)(2,1)S(1)}, u32[]{:S(2)}, u32[]{:S(2)}) collective-permute-start(bf16[192,2,128]{2,1,0:T(2,128)(2,1)S(1)} %get-tuple-element.177), channel_id=1, source_target_pairs={{0,256},{32,288},{64,320},{96,352},{128,384},{160,416},{192,448},{... | collective-permute-start | bytes 294920 | tf_op jit(solution)/shard_map/ppermute | solution.py:26
  228.4 21.9 %collective-permute-start.8 = (bf16[192,2,128]{2,1,0:T(2,128)(2,1)S(1)}, bf16[192,2,128]{2,1,0:T(2,128)(2,1)S(1)}, u32[]{:S(2)}, u32[]{:S(2)}) collective-permute-start(bf16[192,2,128]{2,1,0:T(2,128)(2,1)S(1)} %get-tuple-element.176), channel_id=1, source_target_pairs={{0,288},{32,256},{64,352},{96,320},{128,416},{160,384},{192,480},{... | collective-permute-start | bytes 294920 | tf_op jit(solution)/shard_map/ppermute | solution.py:26
  231.1 24.6 %collective-permute-start.9 = (bf16[192,2,128]{2,1,0:T(2,128)(2,1)S(1)}, bf16[192,2,128]{2,1,0:T(2,128)(2,1)S(1)}, u32[]{:S(2)}, u32[]{:S(2)}) collective-permute-start(bf16[192,2,128]{2,1,0:T(2,128)(2,1)S(1)} %get-tuple-element.175), channel_id=1, source_target_pairs={{0,320},{32,352},{64,256},{96,288},{128,448},{160,480},{192,384},{... | collective-permute-start | bytes 294920 | tf_op jit(solution)/shard_map/ppermute | solution.py:26
  236.6 22.0 %collective-permute-start.10 = (bf16[192,2,128]{2,1,0:T(2,128)(2,1)S(1)}, bf16[192,2,128]{2,1,0:T(2,128)(2,1)S(1)}, u32[]{:S(2)}, u32[]{:S(2)}) collective-permute-start(bf16[192,2,128]{2,1,0:T(2,128)(2,1)S(1)} %get-tuple-element.174), channel_id=1, source_target_pairs={{0,352},{32,320},{64,288},{96,256},{128,480},{160,448},{192,416},{... | collective-permute-start | bytes 294920 | tf_op jit(solution)/shard_map/ppermute | solution.py:26
  241.0 18.2 %collective-permute-start.11 = (bf16[192,2,128]{2,1,0:T(2,128)(2,1)S(1)}, bf16[192,2,128]{2,1,0:T(2,128)(2,1)S(1)}, u32[]{:S(2)}, u32[]{:S(2)}) collective-permute-start(bf16[192,2,128]{2,1,0:T(2,128)(2,1)S(1)} %get-tuple-element.173), channel_id=1, source_target_pairs={{0,384},{32,416},{64,448},{96,480},{128,256},{160,288},{192,320},{... | collective-permute-start | bytes 294920 | tf_op jit(solution)/shard_map/ppermute | solution.py:26
  245.7 14.3 %collective-permute-start.12 = (bf16[192,2,128]{2,1,0:T(2,128)(2,1)S(1)}, bf16[192,2,128]{2,1,0:T(2,128)(2,1)S(1)}, u32[]{:S(2)}, u32[]{:S(2)}) collective-permute-start(bf16[192,2,128]{2,1,0:T(2,128)(2,1)S(1)} %get-tuple-element.172), channel_id=1, source_target_pairs={{0,416},{32,384},{64,480},{96,448},{128,288},{160,256},{192,352},{... | collective-permute-start | bytes 294920 | tf_op jit(solution)/shard_map/ppermute | solution.py:26
  250.2 11.1 %collective-permute-start.13 = (bf16[192,2,128]{2,1,0:T(2,128)(2,1)S(1)}, bf16[192,2,128]{2,1,0:T(2,128)(2,1)S(1)}, u32[]{:S(2)}, u32[]{:S(2)}) collective-permute-start(bf16[192,2,128]{2,1,0:T(2,128)(2,1)S(1)} %get-tuple-element.171), channel_id=1, source_target_pairs={{0,448},{32,480},{64,384},{96,416},{128,320},{160,352},{192,256},{... | collective-permute-start | bytes 294920 | tf_op jit(solution)/shard_map/ppermute | solution.py:26
  255.7 10.1 %collective-permute-start.14 = (bf16[192,2,128]{2,1,0:T(2,128)(2,1)S(1)}, bf16[192,2,128]{2,1,0:T(2,128)(2,1)S(1)}, u32[]{:S(2)}, u32[]{:S(2)}) collective-permute-start(bf16[192,2,128]{2,1,0:T(2,128)(2,1)S(1)} %get-tuple-element.170), channel_id=1, source_target_pairs={{0,480},{32,448},{64,416},{96,384},{128,352},{160,320},{192,288},{... | collective-permute-start | bytes 294920 | tf_op jit(solution)/shard_map/ppermute | solution.py:26
Sparse Core Ops, SparseCore 0:
  665.1 150.8 all-reduce.1
